TPU v7x, 32 devices: a whole 2x2x4 slice. The times are simulated.
32 devices in a mesh: dp: 8 (over z, y), vocab: 4 (over x, core).
Axes of the slice: x: 2, y: 2, z: 4, core: 2. Of those that a mesh axis runs over, the one named last changes fastest.
Arguments:
- hidden_in: bfloat16 [64, 24, 1024], P(('dp', 'vocab')), may hold values from -6 to 6
- tokens: int32 [64, 24], P(('dp', 'vocab')), may hold values from 0 to 131071
- lengths: int32 [64], P(('dp', 'vocab')), may hold values from 2 to 24, as said below
- cutoff: int32 [1], replicated, may hold values from 1 to 64
- norm_gain: float32 [1024], replicated, may hold values from 0.5 to 1.5
- gate_weight: bfloat16 [1024, 4096], P(None, 'vocab'), may hold values from -0.1875 to 0.1875
- up_weight: bfloat16 [1024, 4096], P(None, 'vocab'), may hold values from -0.1875 to 0.1875
- down_weight: bfloat16 [4096, 1024], P('vocab'), may hold values from -0.09375 to 0.09375
- final_gain: float32 [1024], replicated, may hold values from 0.5 to 1.5
- head_table: bfloat16 [131072, 1024], P(('dp', 'vocab')), may hold values from -12 to 12
Outputs:
- log_ppl: float32 [64], P(('dp', 'vocab'))
- margin: float32 [64], P(('dp', 'vocab'))
Inputs may be any that keep to these rules, and one draw needn't show every extreme that they name: Every length is 2 or more; the documents of one device have together at most 32 positions below their lengths, and some device has exactly 32.
All inputs are finite; a program needn't handle non-finite values.
Results may differ from a plain program's by a relative error of at most 0.025.
Values may be sent and summed in bfloat16 or wider, within the bound.
A program may use at most 64 MiB of HBM per device.

v0:
```python
import jax
import jax.numpy as jnp
from jax import lax
from jax.sharding import PartitionSpec as P


def rms_norm(values, gain):
    squares = jnp.mean(values * values, axis=-1, keepdims=True)
    return values * lax.rsqrt(squares + 1e-06) * gain


def block_rows(row_count, shard_rows):
    shards = row_count // shard_rows
    grouped = 1
    for divisor in range(1, shards + 1):
        if shards % divisor == 0 and divisor * shard_rows <= 768:
            grouped = divisor
    return grouped * shard_rows


def make_accumulate(table, offset, shard_rows, model_width):
    column = jnp.arange(table.shape[0], dtype=jnp.int32)

    def score_block(block_pair):
        block_part, block_targets = block_pair
        logits = lax.dot_general(
            block_part, table, (((1,), (1,)), ((), ())), preferred_element_type=jnp.float32
        )
        highest = jnp.max(logits, axis=1)
        exp_sum = jnp.sum(jnp.exp(logits - highest[:, None]), axis=1)
        local_index = block_targets - offset
        picked = jnp.sum(jnp.where(column[None, :] == local_index[:, None], logits, 0.0), axis=1)
        return (highest, exp_sum, picked)

    def accumulate(running, segment, first_row):
        segment_rows, segment_targets = segment
        row_count = segment_rows.shape[0]
        block_size = block_rows(row_count, shard_rows)
        blocks = row_count // block_size
        results = lax.map(
            score_block,
            (
                segment_rows.reshape(blocks, block_size, model_width),
                segment_targets.reshape(blocks, block_size),
            ),
        )
        return tuple((fresh.reshape(row_count) for fresh in results))

    return accumulate


def on_device(
    hidden_in,
    tokens,
    lengths,
    cutoff,
    norm_gain,
    gate_weight,
    up_weight,
    down_weight,
    final_gain,
    head_table,
):
    doc_count, length, model_width = hidden_in.shape
    row_total = doc_count * length
    residual = hidden_in.reshape(row_total, model_width).astype(jnp.float32)
    normed = rms_norm(residual, norm_gain).astype(jnp.bfloat16)
    segment = lax.all_gather(normed, "vocab", axis=0, tiled=True)
    gate_part = jnp.dot(segment, gate_weight, preferred_element_type=jnp.float32)
    up_part = jnp.dot(segment, up_weight, preferred_element_type=jnp.float32)
    active = (jax.nn.silu(gate_part) * up_part).astype(jnp.bfloat16)
    branch = lax.psum_scatter(
        jnp.dot(active, down_weight, preferred_element_type=jnp.float32),
        "vocab",
        scatter_dimension=0,
        tiled=True,
    )
    stream = (residual + branch).astype(jnp.bfloat16)
    final_rows = rms_norm(stream.astype(jnp.float32), final_gain).astype(jnp.bfloat16)
    targets = jnp.concatenate([tokens[:, 1:], tokens[:, :1]], axis=1).reshape(row_total)
    position = jnp.arange(length, dtype=jnp.int32)
    live_mask = (position[None, :] < lengths[:, None] - 1).reshape(row_total)
    vocab_rows = head_table.shape[0]
    shard_rows = final_rows.shape[0]
    offset = lax.axis_index(("dp", "vocab")) * vocab_rows
    accumulate = make_accumulate(head_table, offset, shard_rows, model_width)
    all_rows = shard_rows * lax.axis_size(("dp", "vocab"))
    blank_stats = jnp.zeros((all_rows,), jnp.float32)
    peaks, sums_exp, picks = accumulate(
        (blank_stats, blank_stats, blank_stats),
        (
            lax.all_gather(final_rows, ("dp", "vocab"), axis=0, tiled=True),
            lax.all_gather(targets, ("dp", "vocab"), axis=0, tiled=True),
        ),
        jnp.int32(0),
    )
    grid_shape = (lax.axis_size("dp"), lax.axis_size("vocab"), shard_rows)
    peak_grid, sum_grid, pick_grid = (
        lax.all_to_all(
            lax.all_to_all(
                peaks.reshape(grid_shape), "dp", split_axis=0, concat_axis=0, tiled=True
            ),
            "vocab",
            split_axis=1,
            concat_axis=1,
            tiled=True,
        ),
        lax.all_to_all(
            lax.all_to_all(
                sums_exp.reshape(grid_shape), "dp", split_axis=0, concat_axis=0, tiled=True
            ),
            "vocab",
            split_axis=1,
            concat_axis=1,
            tiled=True,
        ),
        lax.all_to_all(
            lax.all_to_all(
                picks.reshape(grid_shape), "dp", split_axis=0, concat_axis=0, tiled=True
            ),
            "vocab",
            split_axis=1,
            concat_axis=1,
            tiled=True,
        ),
    )
    highest = jnp.max(peak_grid, axis=(0, 1))
    exp_sum = jnp.sum(sum_grid * jnp.exp(peak_grid - highest), axis=(0, 1))
    target_logit = jnp.sum(pick_grid, axis=(0, 1))
    nll_slots = highest + jnp.log(exp_sum) - target_logit
    used_nll = jnp.where(live_mask, nll_slots, 0.0).reshape(doc_count, length)
    log_ppl = jnp.sum(used_nll, axis=1) / (lengths - 1).astype(jnp.float32)
    everyone = lax.all_gather(log_ppl, ("dp", "vocab"), axis=0, tiled=True)
    ordered = jnp.sort(everyone)
    threshold = lax.dynamic_index_in_dim(ordered, cutoff[0] - 1, 0, keepdims=False)
    return (log_ppl, log_ppl - threshold)


def solution(mesh):
    return jax.shard_map(
        on_device,
        mesh=mesh,
        in_specs=(
            P(("dp", "vocab"), None, None),
            P(("dp", "vocab"), None),
            P(("dp", "vocab")),
            P(),
            P(),
            P(None, "vocab"),
            P(None, "vocab"),
            P("vocab", None),
            P(),
            P(("dp", "vocab"), None),
        ),
        out_specs=(P(("dp", "vocab")), P(("dp", "vocab"))),
        check_vma=False,
    )
```

profile of v0, /device:TPU:0, one launch (start us, length us, event | category | flops | bytes accessed | tf_op | source)
XLA Modules:
  0.0 239.4 jit_solution(2721797220075464942)
XLA Ops:
  9.4 7.9 %all_gather.12 = bf16[192,1024]{1,0:T(8,128)(2,1)S(1)} all-gather(bf16[48,1024]{1,0:T(8,128)(2,1)S(1)} %fusion.19), channel_id=1, replica_groups=mesh['dp'=8,'vocab'=4] {'vocab'}, dimensions={0}, use_global_device_ids=true | all-gather | bytes 491520 | tf_op jit(solution)/shard_map/all_gather | solution.py:68
  18.0 4.3 %fusion.7 = f32[192,1024]{1,0:T(8,128)} fusion(bf16[1024,1024]{1,0:T(8,128)(2,1)} %param.19, bf16[192,1024]{1,0:T(8,128)(2,1)S(1)} %all_gather.12, bf16[1024,1024]{1,0:T(8,128)(2,1)} %param.18, f32[192,1024]{1,0:T(8,128)S(1)} %fusion.25), kind=kOutput, calls=%fused_computation.11 | convolution fusion | flops 806486016 | bytes 6160384 | tf_op jit(solution)/shard_map/dot_general | solution.py:73
  22.3 24.2 %reduce-scatter.2.cloned.1.call-done = f32[48,1024]{1,0:T(8,128)} async-done(((f32[192,1024]{1,0:T(8,128)}), f32[48,1024]{1,0:T(8,128)}) %reduce-scatter.2.cloned.1.call-update) | async-done | bytes 196624 | tf_op jit(solution)/shard_map/reduce_scatter | solution.py:72
  47.7 1.6 fusion.16
  49.8 39.5 %all-reduce = s32[1536]{0:T(1024)S(1)} all-reduce(s32[1536]{0:T(1024)S(1)} %dynamic-update-slice), channel_id=1, replica_groups=mesh['dp'=8,'vocab'=4] {'dp','vocab'}, use_global_device_ids=true, to_apply=%add | all-reduce | flops 1536 | bytes 12288
  89.4 19.3 %all-gather.2.cloned.1.call-done = bf16[1536,1024]{1,0:T(8,128)(2,1)} async-done(((bf16[48,1024]{1,0:T(8,128)(2,1)}), bf16[1536,1024]{1,0:T(8,128)(2,1)}) %all-gather.2.cloned.1.call-update) | async-done | bytes 3145744 | tf_op jit(solution)/shard_map/all_gather | solution.py:92
  108.6 28.4 %while.15 = (s32[]{:T(128)}, f32[2,768]{1,0:T(2,128)S(1)}, f32[2,768]{1,0:T(2,128)S(1)}, f32[2,768]{1,0:T(2,128)S(1)}, bf16[2,768,1024]{2,1,0:T(8,128)(2,1)}, /*...) while((s32[]{:T(128)}, f32[2,768]{1,0:T(2,128)S(1)}, ...), condition=%wide.region_7.8_spmd.clone, body=%wide.region_3.7_spmd.clone.sunk | while | flops 6461323776 | bytes 35186296 | solution.py:40
  108.6 9.8 %fusion.35 = (f32[768]{0:T(1024)S(1)}, f32[768,4096]{1,0:T(8,128)S(1)}) fusion(bf16[4096,1024]{1,0:T(8,128)(2,1)} %get-tuple-element.179, bf16[2,768,1024]{2,1,0:T(8,128)(2,1)} %get-tuple-element.178, s32[]{:T(128)} %get-tuple-element.164), kind=kOutput, calls=%fused_computation.42.clone.1 | convolution fusion | flops 6445595648 | bytes 22547968 | tf_op jit(solution)/shard_map/while/body/eval_jaxpr/dot_general | solution.py:26
  118.4 4.2 %select_reduce_fusion.2 = (f32[768]{0:T(1024)S(1)}, f32[768]{0:T(1024)S(1)}) fusion(f32[768,4096]{1,0:T(8,128)S(1)} %get-tuple-element.151, s32[768]{0:T(1024)S(1)} %subtract_reduce_fusion.2, f32[768]{0:T(1024)S(1)} %get-tuple-element.150), kind=kLoop, calls=%fused_computation.2.clone.1 | loop fusion | flops 15727104 | bytes 12595200 | tf_op jit(solution)/shard_map/while/body/eval_jaxpr/reduce_sum | solution.py:32
  122.8 9.8 %fusion.35 = (f32[768]{0:T(1024)S(1)}, f32[768,4096]{1,0:T(8,128)S(1)}) fusion(bf16[4096,1024]{1,0:T(8,128)(2,1)} %get-tuple-element.179, bf16[2,768,1024]{2,1,0:T(8,128)(2,1)} %get-tuple-element.178, s32[]{:T(128)} %get-tuple-element.164), kind=kOutput, calls=%fused_computation.42.clone.1 | convolution fusion | flops 6445595648 | bytes 22547968 | tf_op jit(solution)/shard_map/while/body/eval_jaxpr/dot_general | solution.py:26
  132.7 4.2 %select_reduce_fusion.2 = (f32[768]{0:T(1024)S(1)}, f32[768]{0:T(1024)S(1)}) fusion(f32[768,4096]{1,0:T(8,128)S(1)} %get-tuple-element.151, s32[768]{0:T(1024)S(1)} %subtract_reduce_fusion.2, f32[768]{0:T(1024)S(1)} %get-tuple-element.150), kind=kLoop, calls=%fused_computation.2.clone.1 | loop fusion | flops 15727104 | bytes 12595200 | tf_op jit(solution)/shard_map/while/body/eval_jaxpr/reduce_sum | solution.py:32
  137.8 4.2 %all-to-all-start = ((f32[8,1,192]{2,1,0:T(1,128)}), f32[8,1,192]{2,1,0:T(1,128)S(1)}, u32[]{:S(2)}, u32[]{:S(2)}) async-start(f32[8,1,192]{2,1,0:T(1,128)} %reshape.82), calls=%async_computation.1 | async-start | bytes 16384 | tf_op jit(solution)/shard_map/all_to_all | solution.py:100
  142.8 5.7 %all-to-all-done = f32[8,1,192]{2,1,0:T(1,128)S(1)} async-done(((f32[8,1,192]{2,1,0:T(1,128)}), f32[8,1,192]{2,1,0:T(1,128)S(1)}, u32[]{:S(2)}, u32[]{:S(2)}) %all-to-all-start) | async-done | bytes 6176 | tf_op jit(solution)/shard_map/all_to_all | solution.py:100
  148.6 3.3 %all-to-all-start.2 = ((f32[8,1,192]{2,1,0:T(1,128)}), f32[8,1,192]{2,1,0:T(1,128)S(1)}, u32[]{:S(2)}, u32[]{:S(2)}) async-start(f32[8,1,192]{2,1,0:T(1,128)} %reshape.86), calls=%async_computation.3 | async-start | bytes 16384 | tf_op jit(solution)/shard_map/all_to_all | solution.py:109
  152.7 5.7 %all-to-all-done.2 = f32[8,1,192]{2,1,0:T(1,128)S(1)} async-done(((f32[8,1,192]{2,1,0:T(1,128)}), f32[8,1,192]{2,1,0:T(1,128)S(1)}, u32[]{:S(2)}, u32[]{:S(2)}) %all-to-all-start.2) | async-done | bytes 6176 | tf_op jit(solution)/shard_map/all_to_all | solution.py:109
  158.4 3.3 %all-to-all-start.4 = ((f32[8,1,192]{2,1,0:T(1,128)}), f32[8,1,192]{2,1,0:T(1,128)S(1)}, u32[]{:S(2)}, u32[]{:S(2)}) async-start(f32[8,1,192]{2,1,0:T(1,128)} %reshape.78), calls=%async_computation.5 | async-start | bytes 16384 | tf_op jit(solution)/shard_map/all_to_all | solution.py:118
  163.7 4.5 %all-to-all-done.4 = f32[8,1,192]{2,1,0:T(1,128)S(1)} async-done(((f32[8,1,192]{2,1,0:T(1,128)}), f32[8,1,192]{2,1,0:T(1,128)S(1)}, u32[]{:S(2)}, u32[]{:S(2)}) %all-to-all-start.4) | async-done | bytes 6176 | tf_op jit(solution)/shard_map/all_to_all | solution.py:118
  168.2 3.2 %all-to-all-start.1 = ((f32[4,1,384]{2,1,0:T(1,128)}), f32[4,1,384]{2,1,0:T(1,128)S(1)}, u32[]{:S(2)}, u32[]{:S(2)}) async-start(f32[4,1,384]{2,1,0:T(1,128)} %reshape.84), calls=%async_computation.2 | async-start | bytes 12288 | tf_op jit(solution)/shard_map/all_to_all | solution.py:99
  172.9 2.3 all-to-all-done.1
  175.2 3.2 %all-to-all-start.3 = ((f32[4,1,384]{2,1,0:T(1,128)}), f32[4,1,384]{2,1,0:T(1,128)S(1)}, u32[]{:S(2)}, u32[]{:S(2)}) async-start(f32[4,1,384]{2,1,0:T(1,128)} %reshape.88), calls=%async_computation.4 | async-start | bytes 12288 | tf_op jit(solution)/shard_map/all_to_all | solution.py:108
  182.2 3.2 %all-to-all-start.5 = ((f32[4,1,384]{2,1,0:T(1,128)}), f32[4,1,384]{2,1,0:T(1,128)S(1)}, u32[]{:S(2)}, u32[]{:S(2)}) async-start(f32[4,1,384]{2,1,0:T(1,128)} %reshape.80), calls=%async_computation.6 | async-start | bytes 12288 | tf_op jit(solution)/shard_map/all_to_all | solution.py:117
  186.2 3.0 %all-to-all-done.5 = f32[4,1,384]{2,1,0:T(1,128)S(1)} async-done(((f32[4,1,384]{2,1,0:T(1,128)}), f32[4,1,384]{2,1,0:T(1,128)S(1)}, u32[]{:S(2)}, u32[]{:S(2)}) %all-to-all-start.5) | async-done | bytes 6176 | tf_op jit(solution)/shard_map/all_to_all | solution.py:117
  190.4 38.2 %all-reduce.1 = f32[64]{0:T(128)S(1)} all-reduce(f32[64]{0:T(128)S(1)} %get-tuple-element.93), channel_id=1, replica_groups=mesh['dp'=8,'vocab'=4] {'dp','vocab'}, use_global_device_ids=true, to_apply=%add.1 | all-reduce | flops 64 | bytes 512
  228.6 2.1 sort.15
  (84 shorter events, 17.4 us)
Async XLA Ops:
  7.2 10.2 %copy-start = (bf16[1024,1024]{1,0:T(8,128)(2,1)S(1)}, bf16[1024,1024]{1,0:T(8,128)(2,1)}, u32[]{:S(2)}) copy-start(bf16[1024,1024]{1,0:T(8,128)(2,1)} %param.17) | copy-start | bytes 6291460
  7.2 39.4 %reduce-scatter.2.cloned.1.call-start = ((), (), s32[]{:S(2)}) async-start(), calls=%async_computation.7 | async-start | bytes 983040 | tf_op jit(solution)/shard_map/reduce_scatter | solution.py:72
  18.0 28.6 %copy-start.1 = (bf16[2,24,1024]{2,1,0:T(8,128)(2,1)S(1)}, bf16[2,24,1024]{2,1,0:T(8,128)(2,1)}, u32[]{:S(2)}) copy-start(bf16[2,24,1024]{2,1,0:T(8,128)(2,1)} %param.12) | copy-start | bytes 294916
  18.0 29.7 %copy-start.2 = (f32[1024]{0:T(1024)S(1)}, f32[1024]{0:T(1024)}, u32[]{:S(2)}) copy-start(f32[1024]{0:T(1024)} %param.20) | copy-start | bytes 12292
  18.0 31.4 %copy-start.3 = (s32[2,24]{1,0:T(2,128)S(1)}, s32[2,24]{1,0:T(2,128)}, u32[]{:S(2)}) copy-start(s32[2,24]{1,0:T(2,128)} %param.13) | copy-start | bytes 580
  22.3 86.3 %all-gather.2.cloned.1.call-start = ((), (), s32[]{:S(2)}) async-start(), calls=%async_computation.8 | async-start | bytes 3244032 | tf_op jit(solution)/shard_map/all_gather | solution.py:92
  108.6 69.8 %copy-start.4 = (s32[2]{0:T(128)S(1)}, s32[2]{0:T(128)}, u32[]{:S(2)}) copy-start(s32[2]{0:T(128)} %param.14) | copy-start | bytes 28
  137.8 10.8 %all-to-all-start = ((f32[8,1,192]{2,1,0:T(1,128)}), f32[8,1,192]{2,1,0:T(1,128)S(1)}, u32[]{:S(2)}, u32[]{:S(2)}) async-start(f32[8,1,192]{2,1,0:T(1,128)} %reshape.82), calls=%async_computation.1 | async-start | bytes 16384 | tf_op jit(solution)/shard_map/all_to_all | solution.py:100
  148.6 9.8 %all-to-all-start.2 = ((f32[8,1,192]{2,1,0:T(1,128)}), f32[8,1,192]{2,1,0:T(1,128)S(1)}, u32[]{:S(2)}, u32[]{:S(2)}) async-start(f32[8,1,192]{2,1,0:T(1,128)} %reshape.86), calls=%async_computation.3 | async-start | bytes 16384 | tf_op jit(solution)/shard_map/all_to_all | solution.py:109
  158.4 9.8 %all-to-all-start.4 = ((f32[8,1,192]{2,1,0:T(1,128)}), f32[8,1,192]{2,1,0:T(1,128)S(1)}, u32[]{:S(2)}, u32[]{:S(2)}) async-start(f32[8,1,192]{2,1,0:T(1,128)} %reshape.78), calls=%async_computation.5 | async-start | bytes 16384 | tf_op jit(solution)/shard_map/all_to_all | solution.py:118
  168.2 7.0 %all-to-all-start.1 = ((f32[4,1,384]{2,1,0:T(1,128)}), f32[4,1,384]{2,1,0:T(1,128)S(1)}, u32[]{:S(2)}, u32[]{:S(2)}) async-start(f32[4,1,384]{2,1,0:T(1,128)} %reshape.84), calls=%async_computation.2 | async-start | bytes 12288 | tf_op jit(solution)/shard_map/all_to_all | solution.py:99
  175.2 7.0 %all-to-all-start.3 = ((f32[4,1,384]{2,1,0:T(1,128)}), f32[4,1,384]{2,1,0:T(1,128)S(1)}, u32[]{:S(2)}, u32[]{:S(2)}) async-start(f32[4,1,384]{2,1,0:T(1,128)} %reshape.88), calls=%async_computation.4 | async-start | bytes 12288 | tf_op jit(solution)/shard_map/all_to_all | solution.py:108
  182.2 7.0 %all-to-all-start.5 = ((f32[4,1,384]{2,1,0:T(1,128)}), f32[4,1,384]{2,1,0:T(1,128)S(1)}, u32[]{:S(2)}, u32[]{:S(2)}) async-start(f32[4,1,384]{2,1,0:T(1,128)} %reshape.80), calls=%async_computation.6 | async-start | bytes 12288 | tf_op jit(solution)/shard_map/all_to_all | solution.py:117
  190.4 42.1 %copy-start.5 = (f32[2]{0:T(128)}, f32[2]{0:T(128)S(1)}, u32[]{:S(2)}) copy-start(f32[2]{0:T(128)S(1)} %get-tuple-element.94) | copy-start | bytes 28
Sparse Core Ops, SparseCore 0:
  22.4 24.1 reduce-scatter.1
  49.5 59.1 all-gather.1
where the time goes:
time: 240 us; the launch traced here: 239 us
  blocking collectives  85.6 us (36%)
  waiting for transfers between devices  65.7 us (27%)
  matrix products  24.4 us (10%)
  other arithmetic  21.1 us (9%)
  starting transfers between devices  20.7 us (9%)
  between operations  14.9 us (6%)
  local copies, waits for them, and re-layouts  6.91 us (3%)
    unnamed x2, blocking collectives  77.7 us
    reduce_scatter x1, waiting for transfers between devices, on_device(): lax.psum_scatter(jnp.dot(active, down_weight, preferred_element_type=jnp....  24.2 us
    dot_general x2, matrix products, score_block(): lax.dot_general(block_part, table, (((1,), (1,)), ((), ())), preferred_el...  19.5 us
    all_gather x1, waiting for transfers between devices, on_device(): lax.all_gather(final_rows, ('dp', 'vocab'), axis=0, tiled=True)  19.3 us
    reduce_sum x2, other arithmetic, score_block(): jnp.sum(jnp.where(column[None, :] == local_index[:, None], logits, 0.0),...  8.42 us
    all_gather x1, blocking collectives, on_device(): segment = lax.all_gather(normed, 'vocab', axis=0, tiled=True)  7.93 us
    all_to_all x1, waiting for transfers between devices, on_device(): lax.all_to_all(peaks.reshape(grid_shape), 'dp', split_axis=0, concat_axis...  5.75 us
    all_to_all x1, waiting for transfers between devices, on_device(): lax.all_to_all(sums_exp.reshape(grid_shape), 'dp', split_axis=0, concat_a...  5.68 us
  transfers between devices with their start and end apart: 8, of which 8 were waited for; matrix products, arithmetic and copies ran while one was open for 3% of the time, Pallas kernels for 0%

commit v1 on v0

v1 whole, which is shorter than its diff:
```python
import functools

import jax
import jax.numpy as jnp
from jax import lax
from jax.experimental import pallas as pl
from jax.experimental.pallas import tpu as pltpu
from jax.sharding import PartitionSpec as P

MESH = pl.DeviceIdType.MESH
CAP = 32
LANES = 128


def rms_norm(values, gain):
    squares = jnp.mean(values * values, axis=-1, keepdims=True)
    return values * lax.rsqrt(squares + 1e-06) * gain


def kernel(
    dp_size, vocab_size, docs, length,
    hidden_ref, tokens_ref, lengths_ref, cutoff_ref, norm_gain_ref, final_gain_ref,
    gate_hbm, up_hbm, down_hbm, table_hbm,
    ppl_ref, margin_ref,
    gate, up, down, table, group_rows, acc, part_out, part_in, rows, targets_out, targets_in,
    stats_out, stats_in, ppl_out, ppl_in,
    local_sem, group_send, group_recv, part_send, part_recv, row_send, row_recv,
    target_send, target_recv, stat_send, stat_recv, ppl_send, ppl_recv,
):
    dp = lax.axis_index("dp")
    vocab = lax.axis_index("vocab")
    count = dp_size * vocab_size
    z_size = dp_size // 2
    z, y = dp // 2, dp % 2
    x, c = vocab // 2, vocab % 2
    width = hidden_ref.shape[1]
    vocab_rows = table.shape[0]
    per_lane = LANES // CAP

    def block_of(y, x, c, z):
        return ((y * 2 + x) * 2 + c) * z_size + z

    def device_of(block):
        rest = block // z_size
        return (
            (block % z_size) * 2 + rest // 4,
            ((rest // 2) % 2) * 2 + rest % 2,
        )

    me = block_of(y, x, c, z)
    lane_start = (me % per_lane) * CAP

    local = [
        pltpu.make_async_copy(source, target, local_sem.at[i])
        for i, (source, target) in enumerate(
            ((gate_hbm, gate), (up_hbm, up), (down_hbm, down), (table_hbm, table))
        )
    ]
    for copy in local:
        copy.start()

    barrier = pltpu.get_barrier_semaphore()

    def greet(k, carry):
        pl.semaphore_signal(
            barrier, inc=1, device_id=device_of((me + k) % count), device_id_type=MESH
        )
        return carry

    lax.fori_loop(1, count, greet, 0)

    live = [lengths_ref[i] - 1 for i in range(docs)]
    base = [0]
    for i in range(docs - 1):
        base.append(base[-1] + live[i])
    slot = lax.broadcasted_iota(jnp.int32, (CAP, docs * length), 0)
    position = lax.broadcasted_iota(jnp.int32, (CAP, docs * length), 1)
    chosen = jnp.zeros((CAP, docs * length), jnp.float32)
    lane = lax.broadcasted_iota(jnp.int32, (1, LANES), 1)
    my_slot = lane - lane_start
    target = jnp.zeros((1, LANES), jnp.int32)
    for i in range(docs):
        step = position - i * length
        hit = (step >= 0) & (step < live[i]) & (slot == step + base[i])
        chosen = jnp.where(hit, 1.0, chosen)
        for t in range(length - 1):
            here = (my_slot == base[i] + t) & (t < live[i])
            target = jnp.where(here, tokens_ref[i, t + 1], target)
    packed = jnp.dot(
        chosen.astype(jnp.bfloat16), hidden_ref[...], preferred_element_type=jnp.float32
    )
    group_rows[vocab] = packed.astype(jnp.bfloat16)
    targets_out[...] = target
    targets_in[me] = target

    pl.semaphore_wait(barrier, count - 1)

    def group_copy(buffer_from, buffer_to, send, recv, k):
        other = (vocab + k) % vocab_size
        return pltpu.make_async_remote_copy(
            src_ref=buffer_from(other),
            dst_ref=buffer_to,
            send_sem=send.at[k],
            recv_sem=recv.at[k],
            device_id=(dp, other),
            device_id_type=MESH,
        )

    shares = [
        group_copy(lambda other: group_rows.at[vocab], group_rows.at[vocab], group_send, group_recv, k)
        for k in range(1, vocab_size)
    ]
    for copy in shares:
        copy.start()

    def everyone(source, landing, send, recv):
        def make(k):
            block = (me + k) % count
            return pltpu.make_async_remote_copy(
                src_ref=source(block),
                dst_ref=landing,
                send_sem=send.at[k],
                recv_sem=recv.at[k],
                device_id=device_of(block),
                device_id_type=MESH,
            )

        def start(k, carry):
            make(k).start()
            return carry

        def finish(k, carry):
            make(k).wait()
            return carry

        return start, finish

    target_start, target_finish = everyone(
        lambda block: targets_out, targets_in.at[me], target_send, target_recv
    )
    lax.fori_loop(1, count, target_start, 0)

    for copy in shares:
        copy.wait()
    for copy in local[:3]:
        copy.wait()

    all_rows = vocab_size * CAP
    normed = rms_norm(
        group_rows[...].reshape(all_rows, width).astype(jnp.float32), norm_gain_ref[...]
    ).astype(jnp.bfloat16)
    hidden_units = gate.shape[1]
    tile = min(256, hidden_units)
    for j in range(hidden_units // tile):
        units = pl.ds(j * tile, tile)
        gate_part = jnp.dot(normed, gate[:, units], preferred_element_type=jnp.float32)
        up_part = jnp.dot(normed, up[:, units], preferred_element_type=jnp.float32)
        active = (gate_part / (1.0 + jnp.exp(-gate_part)) * up_part).astype(jnp.bfloat16)
        share = jnp.dot(active, down[units, :], preferred_element_type=jnp.float32)
        if j == 0:
            acc[...] = share
        else:
            acc[...] += share
    part_out[...] = acc[...].reshape(vocab_size, CAP, width).astype(jnp.bfloat16)
    parts = [
        group_copy(lambda other: part_out.at[other], part_in.at[vocab], part_send, part_recv, k)
        for k in range(1, vocab_size)
    ]
    for copy in parts:
        copy.start()
    branch = acc[pl.ds(pl.multiple_of(vocab * CAP, CAP), CAP), :]
    for k, copy in enumerate(parts):
        copy.wait_recv()
        branch = branch + part_in[(vocab + vocab_size - 1 - k) % vocab_size].astype(jnp.float32)
    stream = (packed + branch).astype(jnp.bfloat16).astype(jnp.float32)
    rows[me] = rms_norm(stream, final_gain_ref[...]).astype(jnp.bfloat16)

    pending = []

    def send_row(block, device):
        copy = pltpu.make_async_remote_copy(
            src_ref=rows.at[block],
            dst_ref=rows.at[block],
            send_sem=row_send.at[len(pending)],
            recv_sem=row_recv.at[block],
            device_id=device,
            device_id_type=MESH,
        )
        copy.start()
        pending.append(copy)

    def wait_row(block):
        pltpu.make_async_remote_copy(
            src_ref=rows.at[block],
            dst_ref=rows.at[block],
            send_sem=row_send.at[0],
            recv_sem=row_recv.at[block],
            device_id=(dp, vocab),
            device_id_type=MESH,
        ).wait_recv()

    other_core = (dp, x * 2 + 1 - c)
    y_peer = (z * 2 + 1 - y, vocab)
    x_peer = (dp, (1 - x) * 2 + c)
    half = z_size // 2

    for k in range(1, z_size):
        send_row(me, (((z + k) % z_size) * 2 + y, vocab))
    send_row(me, y_peer)
    send_row(me, x_peer)
    send_row(me, other_core)

    def relay(k):
        there = (z + k) % z_size
        if k:
            block = block_of(y, x, c, there)
            wait_row(block)
            send_row(block, y_peer)
            send_row(block, x_peer)
            send_row(block, other_core)
        block_y = block_of(1 - y, x, c, there)
        wait_row(block_y)
        if k < half:
            send_row(block_y, x_peer)
        send_row(block_y, other_core)
        block_x = block_of(y, 1 - x, c, there)
        wait_row(block_x)
        if k >= half:
            send_row(block_x, y_peer)
        send_row(block_x, other_core)

    def relay_diagonal():
        for k in range(z_size):
            block = block_of(1 - y, 1 - x, c, (z + k) % z_size)
            wait_row(block)
            send_row(block, other_core)

    def wait_core(y, x):
        for k in range(z_size):
            wait_row(block_of(y, x, 1 - c, k))

    offset = (dp * vocab_size + vocab) * vocab_rows
    chunk = min(1024, vocab_rows)
    set_blocks = min(8, 2 * z_size)
    set_rows = set_blocks * CAP
    lane_sets = set_rows // LANES

    def score(y, x):
        def one_set(s, carry):
            first = block_of(y, x, 0, 0) + s * set_blocks
            wanted = jnp.concatenate(
                [
                    jnp.sum(targets_in[pl.ds(first + g * per_lane, per_lane)], axis=0)
                    for g in range(lane_sets)
                ],
                axis=1,
            ) - offset
            sublane = lax.broadcasted_iota(jnp.int32, (8, set_rows), 0)
            wanted = jnp.broadcast_to(wanted, (8, set_rows)) - sublane
            index = lax.broadcasted_iota(jnp.int32, (chunk // 8, 8, set_rows), 0) * 8

            def one_chunk(j, running):
                highest, exp_sum, picked = running
                start = pl.multiple_of(j * chunk, chunk)
                part = rows[pl.ds(first, set_blocks)].reshape(set_rows, width)
                logits = lax.dot_general(
                    table[pl.ds(start, chunk), :],
                    part,
                    (((1,), (1,)), ((), ())),
                    preferred_element_type=jnp.float32,
                ).reshape(chunk // 8, 8, set_rows)
                fresh = jnp.maximum(highest, jnp.max(logits, axis=0))
                exp_sum = exp_sum * jnp.exp(highest - fresh) + jnp.sum(
                    jnp.exp(logits - fresh[None]), axis=0
                )
                picked = picked + jnp.sum(
                    jnp.where(index == (wanted - start)[None], logits, 0.0), axis=0
                )
                return fresh, exp_sum, picked

            blank = jnp.zeros((8, set_rows), jnp.float32)
            highest, exp_sum, picked = lax.fori_loop(
                0, vocab_rows // chunk, one_chunk, (blank - 3e38, blank, blank)
            )
            top = jnp.max(highest, axis=0, keepdims=True)
            total = jnp.sum(exp_sum * jnp.exp(highest - top), axis=0, keepdims=True)
            both = jnp.concatenate(
                [top + jnp.log(total), jnp.sum(picked, axis=0, keepdims=True)], axis=0
            )
            for g in range(lane_sets):
                stats_out[first // per_lane + g] = both[:, g * LANES : (g + 1) * LANES]
            return carry

        lax.fori_loop(0, 2 * z_size // set_blocks, one_set, 0)

    lax.fori_loop(1, count, target_finish, 0)
    for k in range(z_size):
        relay(k)
    local[3].wait()
    wait_core(y, x)
    score(y, x)
    relay_diagonal()
    wait_core(1 - y, x)
    score(1 - y, x)
    wait_core(y, 1 - x)
    score(y, 1 - x)
    wait_core(1 - y, 1 - x)
    score(1 - y, 1 - x)

    stat_start, stat_finish = everyone(
        lambda block: stats_out.at[block // per_lane], stats_in.at[me], stat_send, stat_recv
    )
    lax.fori_loop(1, count, stat_start, 0)
    stats_in[me] = stats_out[me // per_lane]
    for copy in pending:
        copy.wait_send()
    for copy in parts:
        copy.wait_send()
    lax.fori_loop(1, count, stat_finish, 0)

    gathered = stats_in[...]
    shares_lse = gathered[:, 0, :]
    top = jnp.max(shares_lse, axis=0, keepdims=True)
    nll = (
        top
        + jnp.log(jnp.sum(jnp.exp(shares_lse - top), axis=0, keepdims=True))
        - jnp.sum(gathered[:, 1, :], axis=0, keepdims=True)
    )
    doc_lanes = ppl_out.shape[1]
    doc_lane = lax.broadcasted_iota(jnp.int32, (1, doc_lanes), 1)
    mine = jnp.zeros((1, doc_lanes), jnp.float32)
    values = []
    for i in range(docs):
        inside = (my_slot >= base[i]) & (my_slot < base[i] + live[i])
        used = jnp.sum(jnp.where(inside, nll, 0.0), axis=1, keepdims=True)
        value = used / jnp.full((1, 1), live[i], jnp.int32).astype(jnp.float32)
        values.append(value)
        mine = jnp.where(doc_lane == me * docs + i, value, mine)
    ppl_out[...] = mine
    ppl_in[me] = mine
    ppl_start, ppl_finish = everyone(lambda block: ppl_out, ppl_in.at[me], ppl_send, ppl_recv)
    lax.fori_loop(1, count, ppl_start, 0)
    lax.fori_loop(1, count, ppl_finish, 0)

    table_ppl = ppl_in[...].reshape(count, doc_lanes)
    row = jnp.sum(table_ppl, axis=0, keepdims=True)
    source = lax.broadcasted_iota(jnp.int32, (count, doc_lanes), 0)
    lanes = lax.broadcasted_iota(jnp.int32, (count, doc_lanes), 1)
    smaller = jnp.zeros((1, doc_lanes), jnp.float32)
    for i in range(docs):
        column = jnp.sum(
            jnp.where(lanes == source * docs + i, table_ppl, 0.0), axis=1, keepdims=True
        )
        smaller = smaller + jnp.sum(jnp.where(column < row, 1.0, 0.0), axis=0, keepdims=True)
    cutoff = jnp.full((1, doc_lanes), cutoff_ref[0], jnp.int32).astype(jnp.float32)
    allowed = (smaller < cutoff) & (doc_lane < count * docs)
    threshold = jnp.max(jnp.where(allowed, row, -3e38), axis=1, keepdims=True)
    shown = lax.broadcasted_iota(jnp.int32, (1, LANES), 1)
    ppl_row = jnp.zeros((1, LANES), jnp.float32)
    for i in range(docs):
        ppl_row = jnp.where(shown == i, values[i], ppl_row)
    ppl_ref[...] = ppl_row
    margin_ref[...] = ppl_row - threshold


def on_device(
    dp_size, vocab_size,
    hidden_in, tokens, lengths, cutoff, norm_gain,
    gate_weight, up_weight, down_weight, final_gain, head_table,
):
    docs, length, width = hidden_in.shape
    count = dp_size * vocab_size
    doc_lanes = -(-count * docs // LANES) * LANES
    bf16, f32 = jnp.bfloat16, jnp.float32
    vmem = pl.BlockSpec(memory_space=pltpu.VMEM)
    smem = pl.BlockSpec(memory_space=pltpu.SMEM)
    hbm = pl.BlockSpec(memory_space=pl.ANY)
    dma = pltpu.SemaphoreType.DMA
    z_size = dp_size // 2
    row_sends = 8 * z_size + 2 * z_size
    log_ppl, margin = pl.pallas_call(
        functools.partial(kernel, dp_size, vocab_size, docs, length),
        out_shape=(jax.ShapeDtypeStruct((1, LANES), f32),) * 2,
        in_specs=[vmem, smem, smem, smem, vmem, vmem, hbm, hbm, hbm, hbm],
        out_specs=(vmem, vmem),
        scratch_shapes=[
            pltpu.VMEM(gate_weight.shape, bf16),
            pltpu.VMEM(up_weight.shape, bf16),
            pltpu.VMEM(down_weight.shape, bf16),
            pltpu.VMEM(head_table.shape, bf16),
            pltpu.VMEM((vocab_size, CAP, width), bf16),
            pltpu.VMEM((vocab_size * CAP, width), f32),
            pltpu.VMEM((vocab_size, CAP, width), bf16),
            pltpu.VMEM((vocab_size, CAP, width), bf16),
            pltpu.VMEM((count, CAP, width), bf16),
            pltpu.VMEM((1, LANES), jnp.int32),
            pltpu.VMEM((count, 1, LANES), jnp.int32),
            pltpu.VMEM((count * CAP // LANES, 2, LANES), f32),
            pltpu.VMEM((count, 2, LANES), f32),
            pltpu.VMEM((1, doc_lanes), f32),
            pltpu.VMEM((count, 1, doc_lanes), f32),
            dma((4,)),
            dma((vocab_size,)), dma((vocab_size,)),
            dma((vocab_size,)), dma((vocab_size,)),
            dma((row_sends,)), dma((count,)),
            dma((count,)), dma((count,)),
            dma((count,)), dma((count,)),
            dma((count,)), dma((count,)),
        ],
        compiler_params=pltpu.CompilerParams(collective_id=0, has_side_effects=True),
        name="whole_step",
    )(
        hidden_in.reshape(docs * length, width), tokens, lengths, cutoff,
        norm_gain.reshape(1, width), final_gain.reshape(1, width),
        gate_weight, up_weight, down_weight, head_table,
    )
    return log_ppl[0, :docs], margin[0, :docs]


def solution(mesh):
    return jax.shard_map(
        functools.partial(on_device, mesh.shape["dp"], mesh.shape["vocab"]),
        mesh=mesh,
        in_specs=(
            P(("dp", "vocab"), None, None),
            P(("dp", "vocab"), None),
            P(("dp", "vocab")),
            P(),
            P(),
            P(None, "vocab"),
            P(None, "vocab"),
            P("vocab", None),
            P(),
            P(("dp", "vocab"), None),
        ),
        out_specs=(P(("dp", "vocab")), P(("dp", "vocab"))),
        check_vma=False,
    )
```

time: 240 us -> 68.3 us (0.28)
  blocking collectives: 85.6 us -> 0 us
  waiting for transfers between devices: 65.7 us -> 0 us
  Pallas kernels: 0 us -> 65.6 us
  matrix products: 24.4 us -> 0 us
  other arithmetic: 21.1 us -> 0 us
  starting transfers between devices: 20.7 us -> 0 us
  between operations: 14.9 us -> 1.29 us
  local copies, waits for them, and re-layouts: 6.91 us -> 1.19 us
    unnamed x2 -> x0, blocking collectives: 77.7 us -> none
    pallas_call x0 -> x1, Pallas kernels: none -> 65.6 us  [on_device(): pl.pallas_call(functools.partial(kernel, dp_size, vocab_size, docs, lengt...]
    dot_general x4 -> x0, matrix products: 24.4 us -> none  [the longest x2 19.5 us: score_block(): lax.dot_general(block_part, table, (((1,), (1,)), ((), ())), preferred_el...]
    reduce_scatter x1 -> x0, waiting for transfers between devices: 24.2 us -> none  [on_device(): lax.psum_scatter(jnp.dot(active, down_weight, preferred_element_type=jnp....]
    all_to_all x6 -> x0, waiting for transfers between devices: 22.1 us -> none  [the longest x1 5.75 us: on_device(): lax.all_to_all(peaks.reshape(grid_shape), 'dp', split_axis=0, concat_axis...]
    all_to_all x6 -> x0, starting transfers between devices: 20.6 us -> none  [the longest x1 4.24 us: on_device(): lax.all_to_all(peaks.reshape(grid_shape), 'dp', split_axis=0, concat_axis...]
    all_gather x1 -> x0, waiting for transfers between devices: 19.3 us -> none  [on_device(): lax.all_gather(final_rows, ('dp', 'vocab'), axis=0, tiled=True)]
    reduce_sum x7 -> x0, other arithmetic: 10.8 us -> none  [the longest x2 8.42 us: score_block(): jnp.sum(jnp.where(column[None, :] == local_index[:, None], logits, 0.0),...]
  transfers between devices with their start and end apart: 8 -> 0, of which waited for: 8 -> 0; matrix products, arithmetic and copies ran while one was open for 3% -> 0% of each run, Pallas kernels for 0% -> 0%
where the time goes in v1:
time: 68.3 us; the launch traced here: 68.1 us
  Pallas kernels  65.6 us (96%)
  between operations  1.29 us (2%)
  local copies, waits for them, and re-layouts  1.19 us (2%)
    pallas_call x1, Pallas kernels, on_device(): pl.pallas_call(functools.partial(kernel, dp_size, vocab_size, docs, lengt...  65.6 us

profile of v1, /device:TPU:0, one launch (start us, length us, event | category | flops | bytes accessed | tf_op | source)
XLA Modules:
  0.0 68.1 jit_solution(3670713300802897558)
XLA Ops:
  1.3 65.6 %whole_step.1 = (f32[1,128]{1,0:T(1,128)}, f32[1,128]{1,0:T(1,128)}) custom-call(bf16[48,1024]{1,0:T(8,128)(2,1)} %bitcast.7, s32[2,24]{1,0:T(2,128)} %tokens_ref.1, s32[2]{0:T(128)} %lengths_ref.1, s32[1]{0:T(128)S(6)} %copy.12.cutoff_ref, f32[1,1024]{1,0:T(1,128)} %bitcast.8, f32[1,1024]{1,0:T(1,128)} %bitcast.9, bf16[1024,1024]{1,0:T(8,128)(2,1)} %gate_hbm.1, ...), custom_call_target="tpu_custom_call" | custom-call | tf_op jit(solution)/shard_map/whole_step/pallas_call | solution.py:381
  66.9 1.2 %slice_bitcast_fusion = (f32[2]{0:T(128)}, f32[2]{0:T(128)}) fusion(f32[1,128]{1,0:T(1,128)} %get-tuple-element.5, f32[1,128]{1,0:T(1,128)} %get-tuple-element.4), kind=kLoop, calls=%fused_computation | loop fusion | bytes 32 | tf_op jit(solution)/shard_map/squeeze | solution.py:417

commit v2 on v1

--- a/solution.py
+++ b/solution.py
@@ -22,10 +22,10 @@
     hidden_ref, tokens_ref, lengths_ref, cutoff_ref, norm_gain_ref, final_gain_ref,
     gate_hbm, up_hbm, down_hbm, table_hbm,
     ppl_ref, margin_ref,
-    gate, up, down, table, group_rows, acc, part_out, part_in, rows, targets_out, targets_in,
+    gate, up, down, table, group_rows, acc, part_out, part_in, rows,
     stats_out, stats_in, ppl_out, ppl_in,
     local_sem, group_send, group_recv, part_send, part_recv, row_send, row_recv,
-    target_send, target_recv, stat_send, stat_recv, ppl_send, ppl_recv,
+    stat_send, stat_recv, ppl_send, ppl_recv,
 ):
     dp = lax.axis_index("dp")
     vocab = lax.axis_index("vocab")
@@ -61,13 +61,11 @@
 
     barrier = pltpu.get_barrier_semaphore()
 
-    def greet(k, carry):
-        pl.semaphore_signal(
-            barrier, inc=1, device_id=device_of((me + k) % count), device_id_type=MESH
-        )
-        return carry
-
-    lax.fori_loop(1, count, greet, 0)
+    partners = [(dp, (vocab + k) % vocab_size) for k in range(1, vocab_size)]
+    partners += [((z ^ k) * 2 + y, vocab) for k in range(1, z_size)]
+    partners.append((z * 2 + 1 - y, vocab))
+    for device in partners:
+        pl.semaphore_signal(barrier, inc=1, device_id=device, device_id_type=MESH)
 
     live = [lengths_ref[i] - 1 for i in range(docs)]
     base = [0]
@@ -90,10 +88,8 @@
         chosen.astype(jnp.bfloat16), hidden_ref[...], preferred_element_type=jnp.float32
     )
     group_rows[vocab] = packed.astype(jnp.bfloat16)
-    targets_out[...] = target
-    targets_in[me] = target
-
-    pl.semaphore_wait(barrier, count - 1)
+
+    pl.semaphore_wait(barrier, len(partners))
 
     def group_copy(buffer_from, buffer_to, send, recv, k):
         other = (vocab + k) % vocab_size
@@ -134,11 +130,6 @@
             return carry
 
         return start, finish
-
-    target_start, target_finish = everyone(
-        lambda block: targets_out, targets_in.at[me], target_send, target_recv
-    )
-    lax.fori_loop(1, count, target_start, 0)
 
     for copy in shares:
         copy.wait()
@@ -173,7 +164,14 @@
         copy.wait_recv()
         branch = branch + part_in[(vocab + vocab_size - 1 - k) % vocab_size].astype(jnp.float32)
     stream = (packed + branch).astype(jnp.bfloat16).astype(jnp.float32)
-    rows[me] = rms_norm(stream, final_gain_ref[...]).astype(jnp.bfloat16)
+    final = rms_norm(stream, final_gain_ref[...])
+    code = jnp.concatenate(
+        [(lax.shift_right_logical(target, 8 * i) & 255).astype(jnp.float32) for i in range(3)]
+        + [jnp.zeros((1, width - 3 * LANES), jnp.float32)],
+        axis=1,
+    )
+    last = lax.broadcasted_iota(jnp.int32, (CAP, width), 0) == CAP - 1
+    rows[me] = jnp.where(last, code, final).astype(jnp.bfloat16)
 
     pending = []
 
@@ -202,36 +200,36 @@
     other_core = (dp, x * 2 + 1 - c)
     y_peer = (z * 2 + 1 - y, vocab)
     x_peer = (dp, (1 - x) * 2 + c)
-    half = z_size // 2
 
     for k in range(1, z_size):
-        send_row(me, (((z + k) % z_size) * 2 + y, vocab))
-    send_row(me, y_peer)
-    send_row(me, x_peer)
-    send_row(me, other_core)
-
-    def relay(k):
-        there = (z + k) % z_size
-        if k:
-            block = block_of(y, x, c, there)
-            wait_row(block)
-            send_row(block, y_peer)
-            send_row(block, x_peer)
-            send_row(block, other_core)
-        block_y = block_of(1 - y, x, c, there)
+        send_row(me, ((z ^ k) * 2 + y, vocab))
+        if k == 1:
+            send_row(me, y_peer)
+            send_row(me, x_peer)
+            send_row(me, other_core)
+
+    def relay_z(k):
+        block = block_of(y, x, c, z ^ k)
+        wait_row(block)
+        send_row(block, y_peer)
+        send_row(block, x_peer)
+        send_row(block, other_core)
+
+    def relay_sides(k):
+        block_y = block_of(1 - y, x, c, z ^ k)
         wait_row(block_y)
-        if k < half:
+        if k % 2:
             send_row(block_y, x_peer)
         send_row(block_y, other_core)
-        block_x = block_of(y, 1 - x, c, there)
+        block_x = block_of(y, 1 - x, c, z ^ k)
         wait_row(block_x)
-        if k >= half:
+        if k % 2 == 0:
             send_row(block_x, y_peer)
         send_row(block_x, other_core)
 
     def relay_diagonal():
         for k in range(z_size):
-            block = block_of(1 - y, 1 - x, c, (z + k) % z_size)
+            block = block_of(1 - y, 1 - x, c, z ^ k)
             wait_row(block)
             send_row(block, other_core)
 
@@ -245,12 +243,19 @@
     set_rows = set_blocks * CAP
     lane_sets = set_rows // LANES
 
+    def read_targets(first):
+        code = jnp.sum(
+            rows[pl.ds(first, per_lane), CAP - 16 :, : 3 * LANES].astype(jnp.float32), axis=0
+        )[15:, :]
+        low, mid, high = (code[:, i * LANES : (i + 1) * LANES] for i in range(3))
+        return (low + 256.0 * mid + 65536.0 * high).astype(jnp.int32)
+
     def score(y, x):
         def one_set(s, carry):
             first = block_of(y, x, 0, 0) + s * set_blocks
             wanted = jnp.concatenate(
                 [
-                    jnp.sum(targets_in[pl.ds(first + g * per_lane, per_lane)], axis=0)
+                    read_targets(first + g * per_lane)
                     for g in range(lane_sets)
                 ],
                 axis=1,
@@ -293,24 +298,42 @@
 
         lax.fori_loop(0, 2 * z_size // set_blocks, one_set, 0)
 
-    lax.fori_loop(1, count, target_finish, 0)
-    for k in range(z_size):
-        relay(k)
+    stat_start, stat_finish = everyone(
+        lambda block: stats_out.at[block // per_lane], stats_in.at[me], stat_send, stat_recv
+    )
+    chip_blocks = 2 * z_size
+    my_place = me % chip_blocks
+
+    def share_stats(y, x, own):
+        def one(j, carry):
+            block = block_of(y, x, 0, 0) + (my_place + j) % chip_blocks
+            stat_start((block + count - me) % count, 0)
+            return carry
+
+        lax.fori_loop(1 if own else 0, chip_blocks, one, 0)
+
+    relay_z(1)
+    relay_sides(0)
+    relay_sides(1)
+    for k in range(2, z_size):
+        relay_z(k)
     local[3].wait()
     wait_core(y, x)
     score(y, x)
-    relay_diagonal()
+    share_stats(y, x, True)
+    for k in range(2, z_size):
+        relay_sides(k)
     wait_core(1 - y, x)
     score(1 - y, x)
+    share_stats(1 - y, x, False)
+    relay_diagonal()
     wait_core(y, 1 - x)
     score(y, 1 - x)
+    share_stats(y, 1 - x, False)
     wait_core(1 - y, 1 - x)
     score(1 - y, 1 - x)
-
-    stat_start, stat_finish = everyone(
-        lambda block: stats_out.at[block // per_lane], stats_in.at[me], stat_send, stat_recv
-    )
-    lax.fori_loop(1, count, stat_start, 0)
+    share_stats(1 - y, 1 - x, False)
+
     stats_in[me] = stats_out[me // per_lane]
     for copy in pending:
         copy.wait_send()
@@ -393,8 +416,6 @@
             pltpu.VMEM((vocab_size, CAP, width), bf16),
             pltpu.VMEM((vocab_size, CAP, width), bf16),
             pltpu.VMEM((count, CAP, width), bf16),
-            pltpu.VMEM((1, LANES), jnp.int32),
-            pltpu.VMEM((count, 1, LANES), jnp.int32),
             pltpu.VMEM((count * CAP // LANES, 2, LANES), f32),
             pltpu.VMEM((count, 2, LANES), f32),
             pltpu.VMEM((1, doc_lanes), f32),
@@ -403,7 +424,6 @@
             dma((vocab_size,)), dma((vocab_size,)),
             dma((vocab_size,)), dma((vocab_size,)),
             dma((row_sends,)), dma((count,)),
-            dma((count,)), dma((count,)),
             dma((count,)), dma((count,)),
             dma((count,)), dma((count,)),
         ],

time: 68.3 us -> 58.5 us (0.86)
  Pallas kernels: 65.6 us -> 55.8 us
    pallas_call x1, Pallas kernels: 65.6 us -> 55.8 us  [on_device(): pl.pallas_call(functools.partial(kernel, dp_size, vocab_size, docs, lengt...]
where the time goes in v2:
time: 58.5 us; the launch traced here: 58.3 us
  Pallas kernels  55.8 us (95%)
  between operations  1.29 us (2%)
  local copies, waits for them, and re-layouts  1.19 us (2%)
    pallas_call x1, Pallas kernels, on_device(): pl.pallas_call(functools.partial(kernel, dp_size, vocab_size, docs, lengt...  55.8 us
    squeeze x1, local copies, waits for them, and re-layouts, on_device(): return (log_ppl[0, :docs], margin[0, :docs])  1.19 us

profile of v2, /device:TPU:0, one launch (start us, length us, event | category | flops | bytes accessed | tf_op | source)
XLA Modules:
  0.0 58.3 jit_solution(8341032344804554201)
XLA Ops:
  1.3 55.8 %whole_step.1 = (f32[1,128]{1,0:T(1,128)}, f32[1,128]{1,0:T(1,128)}) custom-call(bf16[48,1024]{1,0:T(8,128)(2,1)} %bitcast.7, s32[2,24]{1,0:T(2,128)} %tokens_ref.1, s32[2]{0:T(128)} %lengths_ref.1, s32[1]{0:T(128)S(6)} %copy.12.cutoff_ref, f32[1,1024]{1,0:T(1,128)} %bitcast.8, f32[1,1024]{1,0:T(1,128)} %bitcast.9, bf16[1024,1024]{1,0:T(8,128)(2,1)} %gate_hbm.1, ...), custom_call_target="tpu_custom_call" | custom-call | tf_op jit(solution)/shard_map/whole_step/pallas_call | solution.py:404
  57.1 1.2 %slice_bitcast_fusion = (f32[2]{0:T(128)}, f32[2]{0:T(128)}) fusion(f32[1,128]{1,0:T(1,128)} %get-tuple-element.5, f32[1,128]{1,0:T(1,128)} %get-tuple-element.4), kind=kLoop, calls=%fused_computation | loop fusion | bytes 32 | tf_op jit(solution)/shard_map/squeeze | solution.py:437

commit v3 on v2

--- a/solution.py
+++ b/solution.py
@@ -132,7 +132,7 @@
         return start, finish
 
     for copy in shares:
-        copy.wait()
+        copy.wait_recv()
     for copy in local[:3]:
         copy.wait()
 
@@ -314,14 +314,15 @@
 
     relay_z(1)
     relay_sides(0)
-    relay_sides(1)
     for k in range(2, z_size):
         relay_z(k)
+        if k - 1 < z_size // 2:
+            relay_sides(k - 1)
     local[3].wait()
     wait_core(y, x)
     score(y, x)
     share_stats(y, x, True)
-    for k in range(2, z_size):
+    for k in range(z_size // 2, z_size):
         relay_sides(k)
     wait_core(1 - y, x)
     score(1 - y, x)
@@ -337,7 +338,7 @@
     stats_in[me] = stats_out[me // per_lane]
     for copy in pending:
         copy.wait_send()
-    for copy in parts:
+    for copy in shares + parts:
         copy.wait_send()
     lax.fori_loop(1, count, stat_finish, 0)
 

time: 58.5 us -> 58.4 us (level)
  no operation moved by 1% of the time
where the time goes in v3:
time: 58.4 us; the launch traced here: 58.3 us
  Pallas kernels  55.8 us (96%)
  between operations  1.29 us (2%)
  local copies, waits for them, and re-layouts  1.19 us (2%)
    pallas_call x1, Pallas kernels, on_device(): pl.pallas_call(functools.partial(kernel, dp_size, vocab_size, docs, lengt...  55.8 us
    squeeze x1, local copies, waits for them, and re-layouts, on_device(): return (log_ppl[0, :docs], margin[0, :docs])  1.19 us

profile of v3, /device:TPU:0, one launch (start us, length us, event | category | flops | bytes accessed | tf_op | source)
XLA Modules:
  0.0 58.3 jit_solution(17161596721667588585)
XLA Ops:
  1.3 55.8 %whole_step.1 = (f32[1,128]{1,0:T(1,128)}, f32[1,128]{1,0:T(1,128)}) custom-call(bf16[48,1024]{1,0:T(8,128)(2,1)} %bitcast.7, s32[2,24]{1,0:T(2,128)} %tokens_ref.1, s32[2]{0:T(128)} %lengths_ref.1, s32[1]{0:T(128)S(6)} %copy.12.cutoff_ref, f32[1,1024]{1,0:T(1,128)} %bitcast.8, f32[1,1024]{1,0:T(1,128)} %bitcast.9, bf16[1024,1024]{1,0:T(8,128)(2,1)} %gate_hbm.1, ...), custom_call_target="tpu_custom_call" | custom-call | tf_op jit(solution)/shard_map/whole_step/pallas_call | solution.py:405
  57.1 1.2 %slice_bitcast_fusion = (f32[2]{0:T(128)}, f32[2]{0:T(128)}) fusion(f32[1,128]{1,0:T(1,128)} %get-tuple-element.5, f32[1,128]{1,0:T(1,128)} %get-tuple-element.4), kind=kLoop, calls=%fused_computation | loop fusion | bytes 32 | tf_op jit(solution)/shard_map/squeeze | solution.py:438
